TPU v7x, 256 devices: a whole 4x4x8 slice. The times are simulated.
256 devices in a mesh: expert: 16 (over y, x), tensor: 16 (over z, core).
Axes of the slice: x: 4, y: 4, z: 8, core: 2. Of those that a mesh axis runs over, the one named last changes fastest.
Arguments:
- queries: bfloat16 [4096, 8192], P('expert', 'tensor'), may hold values from -8 to 8
- keys_values: bfloat16 [16, 4, 1280, 256], P('expert'), may hold values from -6 to 6
- prefix_len: int32 [16], P('expert'), may hold values from 128 to 1024, as said below
- out_proj: bfloat16 [8192, 4096], P('tensor', 'expert'), may hold values from -0.0625 to 0.0625
- residual: bfloat16 [4096, 4096], P(('expert', 'tensor')), may hold values from -1.796875 to 1.796875
- norm_gain: float32 [4096], replicated, may hold values from 0.1 to 1.9
- expert_ids: int32 [4096, 8], P('expert'), may hold values from 0 to 63, all different within a row; in each aligned block of 16 rows (0 to 15, 16 to 31, ...) at most 3 rows name the same one
- route_weights: bfloat16 [4096, 8], P('expert'), may hold values from 0.19921875 to 1
- w_gate: bfloat16 [256, 4096, 384], P(('expert', 'tensor')), may hold values from -0.09375 to 0.09375
- w_up: bfloat16 [256, 4096, 384], P(('expert', 'tensor')), may hold values from -0.09375 to 0.09375
- w_down: bfloat16 [256, 384, 4096], P(('expert', 'tensor')), may hold values from -0.15625 to 0.15625
Outputs:
- layer_out: bfloat16 [4096, 4096], P(('expert', 'tensor'))
Inputs may be any that keep to these rules, and one draw needn't show every extreme that they name: `expert_ids`: in the rows of one device (aligned blocks of 16 rows) no expert is named by more than 3 rows, a bound that some block reaches; a row names 8 different experts. `prefix_len`: some sequence has all 1024 slots live.
All inputs are finite; a program needn't handle non-finite values.
Results may differ from a plain program's by a relative error of at most 0.035.
Values may be sent and summed in bfloat16 or wider, within the bound.
No kernel may reach another device: no remote copies, remote signals or barrier semaphores. Data moves between devices by JAX's collectives and lax.ppermute only.
A program may use at most 128 MiB of HBM per device.

v0:
```python
import math
import jax
import jax.numpy as jnp
from jax import lax
from jax.sharding import PartitionSpec as P

HEADS = 64
KVH = 4
HD = 128
TOPK = 8
HSPLIT = 4
TOK_DEV = 16
PREFIX = 1024
MOST = 3
F32 = jnp.float32
BF16 = jnp.bfloat16


def chip_swap(array, tensor_count):
    return lax.ppermute(array, "tensor", [(t, t ^ 1) for t in range(tensor_count)])


def along_z(array, groups):
    return lax.all_to_all(
        array, "tensor", split_axis=0, concat_axis=0, tiled=True, axis_index_groups=groups
    )


def attend(queries, keys_values, prefix_len, kv_index):
    step_rows = queries.shape[0]
    per_device = queries.shape[1] // HD
    cached = lax.dynamic_index_in_dim(keys_values[0], kv_index, 0, keepdims=False)
    key_rows = cached[:, :HD]
    value_rows = cached[:, HD:]
    context = cached.shape[0]
    query_rows = queries.reshape(step_rows, per_device, HD)
    scores = jnp.einsum(
        "nhd,cd->hnc", query_rows, key_rows, preferred_element_type=F32
    ) / math.sqrt(HD)
    columns = jnp.arange(context, dtype=jnp.int32)[None, :]
    positions = jnp.arange(step_rows, dtype=jnp.int32)[:, None]
    visible = ((columns < prefix_len[0]) | (columns >= PREFIX) & (columns - PREFIX <= positions))[
        None
    ]
    highest = jnp.max(jnp.where(visible, scores, -1e30), axis=-1, keepdims=True)
    weights = jnp.exp(jnp.where(visible, scores - highest, -1e30))
    summed = jnp.sum(weights, axis=-1)
    blended = jnp.einsum(
        "hnc,cd->nhd", weights.astype(BF16), value_rows, preferred_element_type=F32
    )
    attended = (blended / jnp.transpose(summed)[:, :, None]).astype(BF16)
    return attended.reshape(step_rows, per_device * HD)


def shards(
    queries,
    keys_values,
    prefix_len,
    out_proj,
    residual,
    norm_gain,
    expert_ids,
    route_weights,
    w_gate,
    w_up,
    w_down,
):
    tensor_count = lax.axis_size("tensor")
    expert_count = lax.axis_size("expert")
    tensor_index = lax.axis_index("tensor")
    chips = tensor_count // 2
    core = tensor_index % 2
    same_core = [[2 * z + c for z in range(chips)] for c in range(2)]
    per_device = queries.shape[1] // HD
    width = residual.shape[1]
    half_rows = chips * TOK_DEV
    gate_other = chip_swap(w_gate[0], tensor_count)
    up_other = chip_swap(w_up[0], tensor_count)
    down_other = chip_swap(w_down[0], tensor_count)
    slot_index = tensor_index // HSPLIT
    slot_count = tensor_count // HSPLIT
    capacity = chips * MOST
    ids = expert_ids.reshape(chips, 2, TOK_DEV, TOPK)
    ids = lax.dynamic_index_in_dim(ids, core, 1, keepdims=False)
    gains = route_weights.reshape(chips, 2, TOK_DEV, TOPK)
    gains = lax.dynamic_index_in_dim(gains, core, 1, keepdims=False)
    wanted = jnp.arange(expert_count, dtype=jnp.int32) * slot_count + slot_index
    named = ids[:, :, :, None] == wanted
    hits = jnp.sum(named.astype(jnp.int32), axis=2)
    weight = jnp.sum(jnp.where(named, gains[:, :, :, None].astype(F32), 0.0), axis=2)
    earlier = (jnp.arange(TOK_DEV)[:, None] > jnp.arange(TOK_DEV)[None, :]).astype(BF16)
    rank = jnp.einsum("nm,zmj->znj", earlier, hits.astype(BF16), preferred_element_type=F32)
    position = jnp.arange(chips, dtype=jnp.int32)[:, None, None] * MOST + rank.astype(jnp.int32)
    position = jnp.where(hits > 0, position, -1).reshape(half_rows, expert_count)
    weight = weight.reshape(half_rows, expert_count)
    slots = jnp.arange(capacity, dtype=jnp.int32)
    pick = (position.T[:, None, :] == slots[None, :, None]).astype(BF16)
    pick = pick.reshape(expert_count * capacity, half_rows)
    combine = jnp.where(position[:, :, None] == slots[None, None, :], weight[:, :, None], 0.0)
    combine = combine.astype(BF16).reshape(half_rows, expert_count * capacity)
    attended = attend(queries, keys_values, prefix_len, tensor_index * per_device // (HEADS // KVH))
    projection = lax.all_gather(out_proj, "expert", axis=1, tiled=True)
    attended = attended.reshape(chips, 2, TOK_DEV, per_device * HD)
    attended_away = lax.dynamic_index_in_dim(attended, 1 - core, 1, keepdims=False)
    attended_here = lax.dynamic_index_in_dim(attended, core, 1, keepdims=False)
    part_away = jnp.dot(
        attended_away.reshape(half_rows, -1), projection, preferred_element_type=F32
    ).astype(BF16)
    part_away = chip_swap(part_away, tensor_count)
    part_here = jnp.dot(
        attended_here.reshape(half_rows, -1), projection, preferred_element_type=F32
    ).astype(BF16)
    chip_part = (part_here.astype(F32) + part_away.astype(F32)).astype(BF16)
    head_parts = along_z(chip_part.reshape(chips, TOK_DEV, width), same_core)
    head_sum = jnp.sum(head_parts.astype(F32), axis=0)
    hidden_state = (residual.astype(F32) + head_sum).astype(BF16)
    values = hidden_state.astype(F32)
    factor = lax.rsqrt(jnp.mean(values * values, axis=-1, keepdims=True) + 1e-06)
    normed = (values * factor * norm_gain[None, :]).astype(BF16)
    normed_half = along_z(jnp.broadcast_to(normed[None], (chips,) + normed.shape), same_core)
    outgoing = jnp.dot(
        pick, normed_half.reshape(half_rows, width), preferred_element_type=F32
    ).astype(BF16)
    arrived = lax.all_to_all(
        outgoing.reshape(expert_count, capacity, width),
        "expert",
        split_axis=0,
        concat_axis=0,
        tiled=True,
    )
    rows = arrived.reshape(expert_count * capacity, width)

    def inner_of(gate, up):
        gate_val = jnp.dot(rows, gate, preferred_element_type=F32)
        up_val = jnp.dot(rows, up, preferred_element_type=F32)
        return (jax.nn.silu(gate_val) * up_val).astype(BF16)

    result = jnp.dot(inner_of(w_gate[0], w_up[0]), w_down[0], preferred_element_type=F32)
    result = result + jnp.dot(
        inner_of(gate_other, up_other), down_other, preferred_element_type=F32
    )
    result = result.astype(BF16).reshape(expert_count, capacity, width)
    returned = lax.all_to_all(result, "expert", split_axis=0, concat_axis=0, tiled=True)
    expert_part = jnp.dot(
        combine, returned.reshape(expert_count * capacity, width), preferred_element_type=F32
    )
    expert_parts = along_z(expert_part.astype(BF16).reshape(chips, TOK_DEV, width), same_core)
    expert_sum = jnp.sum(expert_parts.astype(F32), axis=0)
    return (hidden_state.astype(F32) + expert_sum).astype(BF16)


def solution(mesh):
    return jax.shard_map(
        shards,
        mesh=mesh,
        in_specs=(
            P("expert", "tensor"),
            P("expert", None, None, None),
            P("expert"),
            P("tensor", "expert"),
            P(("expert", "tensor"), None),
            P(),
            P("expert", None),
            P("expert", None),
            P(("expert", "tensor"), None, None),
            P(("expert", "tensor"), None, None),
            P(("expert", "tensor"), None, None),
        ),
        out_specs=P(("expert", "tensor"), None),
        check_vma=False,
    )
```

profile of v0, /device:TPU:24, one launch (start us, length us, event | category | flops | bytes accessed | tf_op | source)
XLA Modules:
  0.0 327.5 jit_solution(82748444382406741)
XLA Ops:
  6.5 0.7 all-gather.2.cloned.1.call-update
  8.3 2.0 fusion.13
  10.4 5.1 %fusion.70 = (f32[4,256]{1,0:T(4,128)S(1)}, bf16[4,256,1280]{1,2,0:T(8,128)(2,1)}) fusion(pred[256,1280]{0,1:T(8,128)(4,1)} %fusion.13, bf16[1280,256]{1,0:T(8,128)(2,1)S(1)} %dynamic-slice_bitcast_fusion, bf16[256,512]{1,0:T(8,128)(2,1)} %param.11), kind=kOutput, calls=%fused_computation.92 | convolution fusion | flops 680264960 | bytes 4460544 | tf_op jit(solution)/shard_map/sub | solution.py:46
  15.5 2.3 fusion.21
  18.1 56.6 %all-gather.2.cloned.1.call-done = bf16[512,4096]{1,0:T(8,128)(2,1)} async-done(((bf16[512,256]{1,0:T(8,128)(2,1)}), bf16[512,4096]{1,0:T(8,128)(2,1)}) %all-gather.2.cloned.1.call-update) | async-done | bytes 4194320 | tf_op jit(solution)/shard_map/all_gather | solution.py:102
  74.7 3.1 convolution_convert_fusion.1
  77.9 2.6 collective-permute-done
  80.5 0.7 add_convert_fusion.1
  81.3 36.0 %all_to_all.25 = bf16[8,16,4096]{2,1,0:T(8,128)(2,1)S(1)} all-to-all(bf16[8,16,4096]{2,1,0:T(8,128)(2,1)S(1)} %bitcast.116), channel_id=1, replica_groups={{0,2,4,6,8,10,12,14},{1,3,5,7,9,11,13,15},{16,18,20,22,24,26,28,30},{17..., dimensions={0} | all-to-all | bytes 2097152 | tf_op jit(solution)/shard_map/all_to_all | solution.py:24
  117.7 1.1 broadcast_in_dim.76
  118.8 4.2 %all-to-all-start.1 = ((bf16[8,16,4096]{2,1,0:T(8,128)(2,1)}), bf16[8,16,4096]{2,1,0:T(8,128)(2,1)}, u32[]{:S(2)}, u32[]{:S(2)}) async-start(bf16[8,16,4096]{2,1,0:T(8,128)(2,1)} %broadcast_in_dim.76), calls=%async_computation.1 | async-start | bytes 2097152 | tf_op jit(solution)/shard_map/all_to_all | solution.py:24
  124.0 26.9 %all-to-all-done.1 = bf16[8,16,4096]{2,1,0:T(8,128)(2,1)} async-done(((bf16[8,16,4096]{2,1,0:T(8,128)(2,1)}), bf16[8,16,4096]{2,1,0:T(8,128)(2,1)}, u32[]{:S(2)}, u32[]{:S(2)}) %all-to-all-start.1) | async-done | bytes 1048608 | tf_op jit(solution)/shard_map/all_to_all | solution.py:24
  150.9 3.8 %convolution_convert_fusion = bf16[384,4096]{1,0:T(8,128)(2,1)} fusion(pred[384,128]{1,0:T(8,128)(4,1)S(1)} %bitcast.122, bf16[128,4096]{1,0:T(8,128)(2,1)} %bitcast.17), kind=kOutput, calls=%fused_computation.2 | convolution fusion | flops 404226048 | bytes 4243456 | tf_op jit(solution)/shard_map/dot_general | solution.py:121
  154.8 5.7 %all-to-all-start.2 = ((bf16[16,24,4096]{2,1,0:T(8,128)(2,1)}), bf16[16,24,4096]{2,1,0:T(8,128)(2,1)}, u32[]{:S(2)}, u32[]{:S(2)}) async-start(bf16[16,24,4096]{2,1,0:T(8,128)(2,1)} %bitcast.114), calls=%async_computation.2 | async-start | bytes 6291456 | tf_op jit(solution)/shard_map/all_to_all | solution.py:124
  161.1 46.1 %all-to-all-done.2 = bf16[16,24,4096]{2,1,0:T(8,128)(2,1)} async-done(((bf16[16,24,4096]{2,1,0:T(8,128)(2,1)}), bf16[16,24,4096]{2,1,0:T(8,128)(2,1)}, u32[]{:S(2)}, u32[]{:S(2)}) %all-to-all-start.2) | async-done | bytes 3145760 | tf_op jit(solution)/shard_map/all_to_all | solution.py:124
  207.2 5.4 %fusion.63 = f32[384,384]{1,0:T(8,128)} fusion(bf16[384,4096]{1,0:T(8,128)(2,1)} %bitcast.19, bf16[1,4096,384]{2,1,0:T(8,128)(2,1)} %param.19), kind=kOutput, calls=%fused_computation.85 | convolution fusion | flops 1207959552 | bytes 6881280 | tf_op jit(solution)/shard_map/dot_general | solution.py:134
  212.7 4.6 %fusion.77 = f32[384,384]{1,0:T(8,128)S(1)} fusion(bf16[384,4096]{1,0:T(8,128)(2,1)} %bitcast.19, bf16[4096,384]{1,0:T(8,128)(2,1)} %collective-permute-done.1), kind=kOutput, calls=%fused_computation.94 | convolution fusion | flops 1207959552 | bytes 6881280 | tf_op jit(solution)/shard_map/dot_general | solution.py:134
  217.3 10.0 %fusion.24 = f32[384,4096]{1,0:T(8,128)} fusion(bf16[384,4096]{1,0:T(8,128)(2,1)} %bitcast.19, f32[384,384]{1,0:T(8,128)} %fusion.63, bf16[1,384,4096]{2,1,0:T(8,128)(2,1)} %param.21, bf16[1,4096,384]{2,1,0:T(8,128)(2,1)} %param.20), kind=kOutput, calls=%fused_computation.30 | convolution fusion | flops 2416803840 | bytes 16318464 | tf_op jit(solution)/shard_map/dot_general | solution.py:138
  227.4 10.7 %add_convert_fusion = bf16[384,4096]{1,0:T(8,128)(2,1)} fusion(f32[384,4096]{1,0:T(8,128)} %fusion.24, bf16[384,4096]{1,0:T(8,128)(2,1)} %collective-permute-done.3, f32[384,384]{1,0:T(8,128)S(1)} %fusion.77, bf16[384,4096]{1,0:T(8,128)(2,1)} %bitcast.19, bf16[4096,384]{1,0:T(8,128)(2,1)} %collective-permute-done.2), kind=kOutput, calls=%fused_computation.1 | convolution fusion | flops 2419949568 | bytes 19464192 | tf_op jit(solution)/shard_map/dot_general | solution.py:139
  238.0 6.0 %all-to-all-start.3 = ((bf16[16,24,4096]{2,1,0:T(8,128)(2,1)}), bf16[16,24,4096]{2,1,0:T(8,128)(2,1)}, u32[]{:S(2)}, u32[]{:S(2)}) async-start(bf16[16,24,4096]{2,1,0:T(8,128)(2,1)} %bitcast.115), calls=%async_computation.3 | async-start | bytes 6291456 | tf_op jit(solution)/shard_map/all_to_all | solution.py:143
  244.7 43.3 %all-to-all-done.3 = bf16[16,24,4096]{2,1,0:T(8,128)(2,1)} async-done(((bf16[16,24,4096]{2,1,0:T(8,128)(2,1)}), bf16[16,24,4096]{2,1,0:T(8,128)(2,1)}, u32[]{:S(2)}, u32[]{:S(2)}) %all-to-all-start.3) | async-done | bytes 3145760 | tf_op jit(solution)/shard_map/all_to_all | solution.py:143
  288.0 2.6 fusion.5
  290.6 29.2 %all_to_all.26 = bf16[8,16,4096]{2,1,0:T(8,128)(2,1)S(1)} all-to-all(bf16[8,16,4096]{2,1,0:T(8,128)(2,1)S(1)} %bitcast.117), channel_id=1, replica_groups={{0,2,4,6,8,10,12,14},{1,3,5,7,9,11,13,15},{16,18,20,22,24,26,28,30},{17..., dimensions={0} | all-to-all | bytes 2097152 | tf_op jit(solution)/shard_map/all_to_all | solution.py:24
  320.0 0.7 fusion.42
  (47 shorter events, 3.4 us)
Async XLA Ops:
  6.5 1.7 copy-start
  6.5 68.2 %all-gather.2.cloned.1.call-start = ((), (), s32[]{:S(2)}) async-start(), calls=%async_computation.5 | async-start | bytes 4456448 | tf_op jit(solution)/shard_map/all_gather | solution.py:102
  74.7 5.8 %copy-start.1 = (bf16[512,4096]{1,0:T(8,128)(2,1)S(1)}, bf16[512,4096]{1,0:T(8,128)(2,1)}, u32[]{:S(2)}) copy-start(bf16[512,4096]{1,0:T(8,128)(2,1)} %all-gather.2.cloned.1.call-done) | copy-start | bytes 12582916
  77.8 2.7 collective-permute-start
  81.2 36.1 %copy-start.2 = (bf16[16,4096]{1,0:T(8,128)(2,1)S(1)}, bf16[16,4096]{1,0:T(8,128)(2,1)}, u32[]{:S(2)}) copy-start(bf16[16,4096]{1,0:T(8,128)(2,1)} %param.15) | copy-start | bytes 393220
  81.3 36.3 %copy-start.3 = (f32[4096]{0:T(1024)S(1)}, f32[4096]{0:T(1024)}, u32[]{:S(2)}) copy-start(f32[4096]{0:T(1024)} %param.16) | copy-start | bytes 49156
  117.2 5.8 %copy-start.4 = (s32[256,8]{0,1:T(8,128)S(1)}, s32[256,8]{0,1:T(8,128)}, u32[]{:S(2)}) copy-start(s32[256,8]{0,1:T(8,128)} %param.17) | copy-start | bytes 24580
  118.8 32.2 %all-to-all-start.1 = ((bf16[8,16,4096]{2,1,0:T(8,128)(2,1)}), bf16[8,16,4096]{2,1,0:T(8,128)(2,1)}, u32[]{:S(2)}, u32[]{:S(2)}) async-start(bf16[8,16,4096]{2,1,0:T(8,128)(2,1)} %broadcast_in_dim.76), calls=%async_computation.1 | async-start | bytes 2097152 | tf_op jit(solution)/shard_map/all_to_all | solution.py:24
  154.8 52.5 %all-to-all-start.2 = ((bf16[16,24,4096]{2,1,0:T(8,128)(2,1)}), bf16[16,24,4096]{2,1,0:T(8,128)(2,1)}, u32[]{:S(2)}, u32[]{:S(2)}) async-start(bf16[16,24,4096]{2,1,0:T(8,128)(2,1)} %bitcast.114), calls=%async_computation.2 | async-start | bytes 6291456 | tf_op jit(solution)/shard_map/all_to_all | solution.py:124
  160.5 52.2 %collective-permute-start.1 = (bf16[4096,384]{1,0:T(8,128)(2,1)}, bf16[4096,384]{1,0:T(8,128)(2,1)}, u32[]{:S(2)}, u32[]{:S(2)}) collective-permute-start(bf16[4096,384]{1,0:T(8,128)(2,1)} %bitcast.127), channel_id=1, source_target_pairs={{0,1},{1,0},{2,3},{3,2},{4,5},{5,4},{6,7},{7,6},{8,9},{9,8},{10,11... | collective-permute-start | bytes 9437192 | tf_op jit(solution)/shard_map/ppermute | solution.py:20
  160.5 66.8 %collective-permute-start.3 = (bf16[384,4096]{1,0:T(8,128)(2,1)}, bf16[384,4096]{1,0:T(8,128)(2,1)}, u32[]{:S(2)}, u32[]{:S(2)}) collective-permute-start(bf16[384,4096]{1,0:T(8,128)(2,1)} %bitcast.118), channel_id=1, source_target_pairs={{0,1},{1,0},{2,3},{3,2},{4,5},{5,4},{6,7},{7,6},{8,9},{9,8},{10,11... | collective-permute-start | bytes 9437192 | tf_op jit(solution)/shard_map/ppermute | solution.py:20
  161.0 66.4 %collective-permute-start.2 = (bf16[4096,384]{1,0:T(8,128)(2,1)}, bf16[4096,384]{1,0:T(8,128)(2,1)}, u32[]{:S(2)}, u32[]{:S(2)}) collective-permute-start(bf16[4096,384]{1,0:T(8,128)(2,1)} %bitcast.119), channel_id=1, source_target_pairs={{0,1},{1,0},{2,3},{3,2},{4,5},{5,4},{6,7},{7,6},{8,9},{9,8},{10,11... | collective-permute-start | bytes 9437192 | tf_op jit(solution)/shard_map/ppermute | solution.py:20
  238.0 6.0 %copy-start.5 = (bf16[256,8]{0,1:T(8,128)(2,1)S(1)}, bf16[256,8]{0,1:T(8,128)(2,1)}, u32[]{:S(2)}) copy-start(bf16[256,8]{0,1:T(8,128)(2,1)} %param.18) | copy-start | bytes 12292
  238.0 50.0 %all-to-all-start.3 = ((bf16[16,24,4096]{2,1,0:T(8,128)(2,1)}), bf16[16,24,4096]{2,1,0:T(8,128)(2,1)}, u32[]{:S(2)}, u32[]{:S(2)}) async-start(bf16[16,24,4096]{2,1,0:T(8,128)(2,1)} %bitcast.115), calls=%async_computation.3 | async-start | bytes 6291456 | tf_op jit(solution)/shard_map/all_to_all | solution.py:143
Sparse Core Ops, SparseCore 0:
  9.8 64.8 all-gather.1
where the time goes:
time: 328 us; the launch traced here: 327 us
  waiting for transfers between devices  176 us (54%)
  blocking collectives  65.2 us (20%)
  matrix products  48.6 us (15%)
  starting transfers between devices  16.7 us (5%)
  between operations  14.4 us (4%)
  other arithmetic  3.96 us (1%)
    all_to_all x2, blocking collectives, along_z(): lax.all_to_all(array, 'tensor', split_axis=0, concat_axis=0, tiled=True,...  65.2 us
    all_gather x1, waiting for transfers between devices, shards(): projection = lax.all_gather(out_proj, 'expert', axis=1, tiled=True)  56.6 us
    all_to_all x1, waiting for transfers between devices, shards(): lax.all_to_all(outgoing.reshape(expert_count, capacity, width), 'expert',...  46.1 us
    all_to_all x1, waiting for transfers between devices, shards(): lax.all_to_all(result, 'expert', split_axis=0, concat_axis=0, tiled=True)  43.3 us
    all_to_all x1, waiting for transfers between devices, along_z(): lax.all_to_all(array, 'tensor', split_axis=0, concat_axis=0, tiled=True,...  26.9 us
    dot_general x1, matrix products, shards(): jnp.dot(inner_of(gate_other, up_other), down_other, preferred_element_typ...  10.7 us
    dot_general x2, matrix products, inner_of(): gate_val = jnp.dot(rows, gate, preferred_element_type=F32)  10.1 us
    dot_general x1, matrix products, shards(): jnp.dot(inner_of(w_gate[0], w_up[0]), w_down[0], preferred_element_type=F32)  10 us
  transfers between devices with their start and end apart: 8, of which 5 were waited for; matrix products, arithmetic and copies ran while one was open for 10% of the time, Pallas kernels for 0%

commit v1 on v0

--- a/solution.py
+++ b/solution.py
@@ -3,6 +3,7 @@
 import jax.numpy as jnp
 from jax import lax
 from jax.sharding import PartitionSpec as P
+from jax.lax import all_to_all, axis_size
 
 HEADS = 64
 KVH = 4
@@ -99,7 +100,11 @@
     combine = jnp.where(position[:, :, None] == slots[None, None, :], weight[:, :, None], 0.0)
     combine = combine.astype(BF16).reshape(half_rows, expert_count * capacity)
     attended = attend(queries, keys_values, prefix_len, tensor_index * per_device // (HEADS // KVH))
-    projection = lax.all_gather(out_proj, "expert", axis=1, tiled=True)
+    views = []
+    for _ in range(axis_size("expert")):
+        views.append(out_proj)
+    p_next = jnp.concatenate(views, 1)
+    projection = all_to_all(p_next, "expert", concat_axis=1, split_axis=1, tiled=True)
     attended = attended.reshape(chips, 2, TOK_DEV, per_device * HD)
     attended_away = lax.dynamic_index_in_dim(attended, 1 - core, 1, keepdims=False)
     attended_here = lax.dynamic_index_in_dim(attended, core, 1, keepdims=False)

time: 328 us -> 334 us (1.018)
  local copies, waits for them, and re-layouts: 2.39 us -> 18.5 us
  between operations: 14.4 us -> 1.11 us
  starting transfers between devices: 16.7 us -> 23.4 us
    all_gather x1 -> x0, waiting for transfers between devices: 56.6 us -> none  [shards(): projection = lax.all_gather(out_proj, 'expert', axis=1, tiled=True)]
    all_to_all x0 -> x1, waiting for transfers between devices: none -> 53.7 us  [shards(): all_to_all(p_next, 'expert', concat_axis=1, split_axis=1, tiled=True)]
    all_to_all x0 -> x2, local copies, waits for them, and re-layouts: none -> 12.9 us  [shards(): all_to_all(p_next, 'expert', concat_axis=1, split_axis=1, tiled=True)]
    all_to_all x0 -> x1, starting transfers between devices: none -> 7.3 us  [shards(): all_to_all(p_next, 'expert', concat_axis=1, split_axis=1, tiled=True)]
  transfers between devices with their start and end apart: 8 -> 8, of which waited for: 5 -> 5; matrix products, arithmetic and copies ran while one was open for 10% -> 8% of each run, Pallas kernels for 0% -> 0%
where the time goes in v1:
time: 334 us; the launch traced here: 333 us
  waiting for transfers between devices  173 us (52%)
  blocking collectives  66.9 us (20%)
  matrix products  46.6 us (14%)
  starting transfers between devices  23.4 us (7%)
  local copies, waits for them, and re-layouts  18.5 us (6%)
    all_to_all x2, blocking collectives, along_z(): lax.all_to_all(array, 'tensor', split_axis=0, concat_axis=0, tiled=True,...  66.9 us
    all_to_all x1, waiting for transfers between devices, shards(): all_to_all(p_next, 'expert', concat_axis=1, split_axis=1, tiled=True)  53.7 us
    all_to_all x1, waiting for transfers between devices, shards(): lax.all_to_all(outgoing.reshape(expert_count, capacity, width), 'expert',...  46.3 us
    all_to_all x1, waiting for transfers between devices, shards(): lax.all_to_all(result, 'expert', split_axis=0, concat_axis=0, tiled=True)  43.8 us
    all_to_all x1, waiting for transfers between devices, along_z(): lax.all_to_all(array, 'tensor', split_axis=0, concat_axis=0, tiled=True,...  26.8 us
    all_to_all x2, local copies, waits for them, and re-layouts, shards(): all_to_all(p_next, 'expert', concat_axis=1, split_axis=1, tiled=True)  12.9 us
    dot_general x1, matrix products, shards(): jnp.dot(inner_of(gate_other, up_other), down_other, preferred_element_typ...  10.7 us
    dot_general x1, matrix products, shards(): jnp.dot(inner_of(w_gate[0], w_up[0]), w_down[0], preferred_element_type=F32)  9.87 us
  transfers between devices with their start and end apart: 8, of which 5 were waited for; matrix products, arithmetic and copies ran while one was open for 8% of the time, Pallas kernels for 0%

profile of v1, /device:TPU:24, one launch (start us, length us, event | category | flops | bytes accessed | tf_op | source)
XLA Modules:
  0.0 332.8 jit_solution(3476188151573780845)
XLA Ops:
  1.7 1.9 copy-done.3
  3.6 6.4 %copy.85 = bf16[512,16,256]{2,0,1:T(8,128)(2,1)} copy(bf16[512,16,256]{0,2,1:T(8,128)(2,1)} %bitcast.120) | data formatting | bytes 8388608 | tf_op jit(solution)/shard_map/all_to_all | solution.py:107
  10.1 7.3 %all-to-all-start = ((bf16[512,16,256]{2,0,1:T(8,128)(2,1)}), bf16[512,16,256]{2,0,1:T(8,128)(2,1)}, u32[]{:S(2)}, u32[]{:S(2)}) async-start(bf16[512,16,256]{2,0,1:T(8,128)(2,1)} %copy.85), calls=%async_computation | async-start | bytes 8388608 | tf_op jit(solution)/shard_map/all_to_all | solution.py:107
  19.2 3.9 %fusion.70 = (f32[4,256]{1,0:T(4,128)S(1)}, bf16[4,256,1280]{1,2,0:T(8,128)(2,1)}) fusion(pred[256,1280]{0,1:T(8,128)(4,1)S(1)} %fusion.13, bf16[1280,256]{1,0:T(8,128)(2,1)S(1)} %dynamic-slice_bitcast_fusion, bf16[256,512]{1,0:T(8,128)(2,1)S(1)} %copy-done.8), kind=kOutput, calls=%fused_computation.108 | convolution fusion | flops 680264960 | bytes 4460544 | tf_op jit(solution)/shard_map/sub | solution.py:47
  23.0 2.3 fusion.21
  25.6 53.7 %all-to-all-done = bf16[512,16,256]{2,0,1:T(8,128)(2,1)} async-done(((bf16[512,16,256]{2,0,1:T(8,128)(2,1)}), bf16[512,16,256]{2,0,1:T(8,128)(2,1)}, u32[]{:S(2)}, u32[]{:S(2)}) %all-to-all-start) | async-done | bytes 4194336 | tf_op jit(solution)/shard_map/all_to_all | solution.py:107
  79.4 6.4 %copy.86 = bf16[512,16,256]{0,2,1:T(8,128)(2,1)} copy(bf16[512,16,256]{2,0,1:T(8,128)(2,1)} %all-to-all-done) | data formatting | bytes 8388608 | tf_op jit(solution)/shard_map/all_to_all | solution.py:107
  85.8 3.8 %convolution_convert_fusion.1 = bf16[128,4096]{1,0:T(8,128)(2,1)S(1)} fusion(bf16[128,512]{1,0:T(8,128)(2,1)S(1)} %bitcast.127, bf16[512,4096]{0,1:T(8,128)(2,1)} %bitcast.116), kind=kOutput, calls=%fused_computation.11 | convolution fusion | flops 537395200 | bytes 5373952 | tf_op jit(solution)/shard_map/dot_general | solution.py:111
  89.7 2.6 collective-permute-done
  92.4 1.5 add_convert_fusion.1
  93.9 37.3 %all_to_all.37 = bf16[8,16,4096]{2,1,0:T(8,128)(2,1)S(1)} all-to-all(bf16[8,16,4096]{2,1,0:T(8,128)(2,1)S(1)} %bitcast.121), channel_id=1, replica_groups={{0,2,4,6,8,10,12,14},{1,3,5,7,9,11,13,15},{16,18,20,22,24,26,28,30},{17..., dimensions={0} | all-to-all | bytes 2097152 | tf_op jit(solution)/shard_map/all_to_all | solution.py:25
  132.7 3.6 %all-to-all-start.2 = ((bf16[8,16,4096]{2,1,0:T(8,128)(2,1)}), bf16[8,16,4096]{2,1,0:T(8,128)(2,1)S(1)}, u32[]{:S(2)}, u32[]{:S(2)}) async-start(bf16[8,16,4096]{2,1,0:T(8,128)(2,1)} %broadcast_in_dim.76), calls=%async_computation.2 | async-start | bytes 2097152 | tf_op jit(solution)/shard_map/all_to_all | solution.py:25
  137.2 26.8 %all-to-all-done.2 = bf16[8,16,4096]{2,1,0:T(8,128)(2,1)S(1)} async-done(((bf16[8,16,4096]{2,1,0:T(8,128)(2,1)}), bf16[8,16,4096]{2,1,0:T(8,128)(2,1)S(1)}, u32[]{:S(2)}, u32[]{:S(2)}) %all-to-all-start.2) | async-done | bytes 1048608 | tf_op jit(solution)/shard_map/all_to_all | solution.py:25
  164.1 2.6 convolution_convert_fusion
  166.7 5.9 %all-to-all-start.3 = ((bf16[16,24,4096]{2,1,0:T(8,128)(2,1)}), bf16[16,24,4096]{2,1,0:T(8,128)(2,1)}, u32[]{:S(2)}, u32[]{:S(2)}) async-start(bf16[16,24,4096]{2,1,0:T(8,128)(2,1)} %bitcast.118), calls=%async_computation.3 | async-start | bytes 6291456 | tf_op jit(solution)/shard_map/all_to_all | solution.py:129
  173.2 46.3 %all-to-all-done.3 = bf16[16,24,4096]{2,1,0:T(8,128)(2,1)} async-done(((bf16[16,24,4096]{2,1,0:T(8,128)(2,1)}), bf16[16,24,4096]{2,1,0:T(8,128)(2,1)}, u32[]{:S(2)}, u32[]{:S(2)}) %all-to-all-start.3) | async-done | bytes 3145760 | tf_op jit(solution)/shard_map/all_to_all | solution.py:129
  219.5 4.6 %fusion.63 = f32[384,384]{1,0:T(8,128)S(1)} fusion(bf16[384,4096]{1,0:T(8,128)(2,1)} %bitcast.21, bf16[1,4096,384]{2,1,0:T(8,128)(2,1)} %param.19), kind=kOutput, calls=%fused_computation.101 | convolution fusion | flops 1207959552 | bytes 6881280 | tf_op jit(solution)/shard_map/dot_general | solution.py:139
  224.1 4.6 %fusion.77 = f32[384,384]{1,0:T(8,128)S(1)} fusion(bf16[384,4096]{1,0:T(8,128)(2,1)} %bitcast.21, bf16[4096,384]{1,0:T(8,128)(2,1)} %collective-permute-done.1), kind=kOutput, calls=%fused_computation.110 | convolution fusion | flops 1207959552 | bytes 6881280 | tf_op jit(solution)/shard_map/dot_general | solution.py:139
  228.7 9.9 %fusion.24 = f32[384,4096]{1,0:T(8,128)} fusion(bf16[384,4096]{1,0:T(8,128)(2,1)} %bitcast.21, f32[384,384]{1,0:T(8,128)S(1)} %fusion.63, bf16[1,384,4096]{2,1,0:T(8,128)(2,1)} %param.21, bf16[1,4096,384]{2,1,0:T(8,128)(2,1)} %param.20), kind=kOutput, calls=%fused_computation.30 | convolution fusion | flops 2416803840 | bytes 16318464 | tf_op jit(solution)/shard_map/dot_general | solution.py:143
  238.6 10.7 %add_convert_fusion = bf16[384,4096]{1,0:T(8,128)(2,1)} fusion(f32[384,4096]{1,0:T(8,128)} %fusion.24, bf16[384,4096]{1,0:T(8,128)(2,1)} %collective-permute-done.3, f32[384,384]{1,0:T(8,128)S(1)} %fusion.77, bf16[384,4096]{1,0:T(8,128)(2,1)} %bitcast.21, bf16[4096,384]{1,0:T(8,128)(2,1)} %collective-permute-done.2), kind=kOutput, calls=%fused_computation.1 | convolution fusion | flops 2419949568 | bytes 19464192 | tf_op jit(solution)/shard_map/dot_general | solution.py:144
  249.3 6.0 %all-to-all-start.4 = ((bf16[16,24,4096]{2,1,0:T(8,128)(2,1)}), bf16[16,24,4096]{2,1,0:T(8,128)(2,1)}, u32[]{:S(2)}, u32[]{:S(2)}) async-start(bf16[16,24,4096]{2,1,0:T(8,128)(2,1)} %bitcast.119), calls=%async_computation.4 | async-start | bytes 6291456 | tf_op jit(solution)/shard_map/all_to_all | solution.py:148
  255.9 43.8 %all-to-all-done.4 = bf16[16,24,4096]{2,1,0:T(8,128)(2,1)} async-done(((bf16[16,24,4096]{2,1,0:T(8,128)(2,1)}), bf16[16,24,4096]{2,1,0:T(8,128)(2,1)}, u32[]{:S(2)}, u32[]{:S(2)}) %all-to-all-start.4) | async-done | bytes 3145760 | tf_op jit(solution)/shard_map/all_to_all | solution.py:148
  299.7 2.6 fusion.5
  302.3 29.6 %all_to_all.38 = bf16[8,16,4096]{2,1,0:T(8,128)(2,1)S(1)} all-to-all(bf16[8,16,4096]{2,1,0:T(8,128)(2,1)S(1)} %bitcast.122), channel_id=1, replica_groups={{0,2,4,6,8,10,12,14},{1,3,5,7,9,11,13,15},{16,18,20,22,24,26,28,30},{17..., dimensions={0} | all-to-all | bytes 2097152 | tf_op jit(solution)/shard_map/all_to_all | solution.py:25
  (71 shorter events, 7.5 us)
Async XLA Ops:
  0.0 18.0 %copy-start = (bf16[1,4,1280,256]{3,2,1,0:T(8,128)(2,1)S(1)}, bf16[1,4,1280,256]{3,2,1,0:T(8,128)(2,1)}, u32[]{:S(2)}) copy-start(bf16[1,4,1280,256]{3,2,1,0:T(8,128)(2,1)} %param.12) | copy-start | bytes 7864324
  1.7 1.9 copy-start.3
  10.0 9.1 %copy-start.8 = (bf16[256,512]{1,0:T(8,128)(2,1)S(1)}, bf16[256,512]{1,0:T(8,128)(2,1)}, u32[]{:S(2)}) copy-start(bf16[256,512]{1,0:T(8,128)(2,1)} %param.11) | copy-start | bytes 786436
  10.1 69.3 %all-to-all-start = ((bf16[512,16,256]{2,0,1:T(8,128)(2,1)}), bf16[512,16,256]{2,0,1:T(8,128)(2,1)}, u32[]{:S(2)}, u32[]{:S(2)}) async-start(bf16[512,16,256]{2,0,1:T(8,128)(2,1)} %copy.85), calls=%async_computation | async-start | bytes 8388608 | tf_op jit(solution)/shard_map/all_to_all | solution.py:107
  85.8 6.6 %copy-start.2 = (bf16[512,16,256]{0,2,1:T(8,128)(2,1)S(1)}, bf16[512,16,256]{0,2,1:T(8,128)(2,1)}, u32[]{:S(2)}) copy-start(bf16[512,16,256]{0,2,1:T(8,128)(2,1)} %copy.86) | copy-start | bytes 12582916
  89.6 2.7 collective-permute-start
  92.4 39.0 %copy-start.4 = (bf16[16,4096]{1,0:T(8,128)(2,1)S(1)}, bf16[16,4096]{1,0:T(8,128)(2,1)}, u32[]{:S(2)}) copy-start(bf16[16,4096]{1,0:T(8,128)(2,1)} %param.15) | copy-start | bytes 393220
  92.4 39.1 %copy-start.5 = (f32[4096]{0:T(1024)S(1)}, f32[4096]{0:T(1024)}, u32[]{:S(2)}) copy-start(f32[4096]{0:T(1024)} %param.16) | copy-start | bytes 49156
  93.9 42.4 %copy-start.6 = (s32[256,8]{0,1:T(8,128)S(1)}, s32[256,8]{0,1:T(8,128)}, u32[]{:S(2)}) copy-start(s32[256,8]{0,1:T(8,128)} %param.17) | copy-start | bytes 24580
  132.7 31.4 %all-to-all-start.2 = ((bf16[8,16,4096]{2,1,0:T(8,128)(2,1)}), bf16[8,16,4096]{2,1,0:T(8,128)(2,1)S(1)}, u32[]{:S(2)}, u32[]{:S(2)}) async-start(bf16[8,16,4096]{2,1,0:T(8,128)(2,1)} %broadcast_in_dim.76), calls=%async_computation.2 | async-start | bytes 2097152 | tf_op jit(solution)/shard_map/all_to_all | solution.py:25
  166.7 52.8 %all-to-all-start.3 = ((bf16[16,24,4096]{2,1,0:T(8,128)(2,1)}), bf16[16,24,4096]{2,1,0:T(8,128)(2,1)}, u32[]{:S(2)}, u32[]{:S(2)}) async-start(bf16[16,24,4096]{2,1,0:T(8,128)(2,1)} %bitcast.118), calls=%async_computation.3 | async-start | bytes 6291456 | tf_op jit(solution)/shard_map/all_to_all | solution.py:129
  172.6 51.5 %collective-permute-start.1 = (bf16[4096,384]{1,0:T(8,128)(2,1)}, bf16[4096,384]{1,0:T(8,128)(2,1)}, u32[]{:S(2)}, u32[]{:S(2)}) collective-permute-start(bf16[4096,384]{1,0:T(8,128)(2,1)} %bitcast.133), channel_id=1, source_target_pairs={{0,1},{1,0},{2,3},{3,2},{4,5},{5,4},{6,7},{7,6},{8,9},{9,8},{10,11... | collective-permute-start | bytes 9437192 | tf_op jit(solution)/shard_map/ppermute | solution.py:21
  172.6 66.0 %collective-permute-start.3 = (bf16[384,4096]{1,0:T(8,128)(2,1)}, bf16[384,4096]{1,0:T(8,128)(2,1)}, u32[]{:S(2)}, u32[]{:S(2)}) collective-permute-start(bf16[384,4096]{1,0:T(8,128)(2,1)} %bitcast.124), channel_id=1, source_target_pairs={{0,1},{1,0},{2,3},{3,2},{4,5},{5,4},{6,7},{7,6},{8,9},{9,8},{10,11... | collective-permute-start | bytes 9437192 | tf_op jit(solution)/shard_map/ppermute | solution.py:21
  173.1 65.5 %collective-permute-start.2 = (bf16[4096,384]{1,0:T(8,128)(2,1)}, bf16[4096,384]{1,0:T(8,128)(2,1)}, u32[]{:S(2)}, u32[]{:S(2)}) collective-permute-start(bf16[4096,384]{1,0:T(8,128)(2,1)} %bitcast.125), channel_id=1, source_target_pairs={{0,1},{1,0},{2,3},{3,2},{4,5},{5,4},{6,7},{7,6},{8,9},{9,8},{10,11... | collective-permute-start | bytes 9437192 | tf_op jit(solution)/shard_map/ppermute | solution.py:21
  249.3 6.0 %copy-start.7 = (bf16[256,8]{0,1:T(8,128)(2,1)S(1)}, bf16[256,8]{0,1:T(8,128)(2,1)}, u32[]{:S(2)}) copy-start(bf16[256,8]{0,1:T(8,128)(2,1)} %param.18) | copy-start | bytes 12292
  249.3 50.4 %all-to-all-start.4 = ((bf16[16,24,4096]{2,1,0:T(8,128)(2,1)}), bf16[16,24,4096]{2,1,0:T(8,128)(2,1)}, u32[]{:S(2)}, u32[]{:S(2)}) async-start(bf16[16,24,4096]{2,1,0:T(8,128)(2,1)} %bitcast.119), calls=%async_computation.4 | async-start | bytes 6291456 | tf_op jit(solution)/shard_map/all_to_all | solution.py:148
  255.4 77.4 %copy-start.1 = (bf16[1,4,1280,256]{3,2,1,0:T(8,128)(2,1)S(1)}, bf16[1,4,1280,256]{3,2,1,0:T(8,128)(2,1)}, u32[]{:S(2)}) copy-start(bf16[1,4,1280,256]{3,2,1,0:T(8,128)(2,1)} %param.12) | copy-start | bytes 7864324
